TPU v7x, 32 devices: a whole 2x2x4 slice. The times are simulated.
32 devices in a mesh: tile: 8 (over y, x, core), chan: 4 (over z).
Axes of the slice: x: 2, y: 2, z: 4, core: 2. Of those that a mesh axis runs over, the one named last changes fastest.
Arguments:
- ensemble: bfloat16 [3072, 128, 256], P('tile', 'chan'), may hold values from -6 to 6
- jacobian: bfloat16 [1280, 128, 128], P('tile', 'chan'), may hold values from -1 to 1
- innovation: float32 [1280, 128], P('tile', 'chan'), may hold values from -6 to 6
- error_vectors: float32 [128, 32], replicated, may hold values from -1 to 1, as said below
- error_values: float32 [128], replicated, may hold values from 0.25 to 4
- ensemble_vectors: float32 [256, 256], replicated, may hold values from -1 to 1, as said below
- column_pick: int32 [8, 5, 40], P('tile'), may hold values from 0 to 383
- footprint_slot: int32 [1280], P('tile'), may hold values from 0 to 199, as said below
- footprint_count: int32 [8], P('tile'), may hold values from 20 to 160, as said below
Outputs:
- analysis: bfloat16 [3072, 128, 256], P('tile', 'chan')
Inputs may be any that keep to these rules, and one draw needn't show every extreme that they name: `footprint_slot`: the 160 entries of one pack are distinct; slot o * 40 + j is the j-th column that tile (pack + 2 - o) mod 8 sends to this pack. `footprint_count`: some pack has all 160 footprints live. `error_vectors`: each block of 32 rows is an orthogonal matrix. `ensemble_vectors`: an orthogonal matrix.
All inputs are finite; a program needn't handle non-finite values.
Results may differ from a plain program's by a relative error of at most 0.013.
Values may be sent and summed in bfloat16 or wider, within the bound.
A program may use at most 64 MiB of HBM per device.

v0:
```python
import jax
import jax.numpy as jnp
from jax import lax
from jax.sharding import PartitionSpec as P


def from_behind(value, axis, steps):
    count = lax.axis_size(axis)
    pairs = [(source, (source + steps) % count) for source in range(count)]
    return lax.ppermute(value, axis, pairs)


def turn_blocks(values, vectors):
    row_count, channels, members = values.shape
    group_width = vectors.shape[1]
    grouped = values.reshape(row_count, channels // group_width, group_width, members)
    basis_blocks = vectors.reshape(channels // group_width, group_width, group_width)
    turned = jnp.einsum("gce,fgck->fgek", basis_blocks, grouped, precision=lax.Precision.HIGHEST)
    return turned.reshape(row_count, channels, members)


def turn_rows(values, vectors):
    row_count, channels = values.shape
    group_width = vectors.shape[1]
    grouped = values.reshape(row_count, channels // group_width, group_width)
    basis_blocks = vectors.reshape(channels // group_width, group_width, group_width)
    turned = jnp.einsum("gce,fgc->fge", basis_blocks, grouped, precision=lax.Precision.HIGHEST)
    return turned.reshape(row_count, channels)


def local(
    ensemble,
    jacobian,
    innovation,
    error_vectors,
    error_values,
    ensemble_vectors,
    column_pick,
    footprint_slot,
    footprint_count,
):
    window = column_pick.shape[1]
    capacity = column_pick.shape[2]
    reach_tiles = window // 2
    level_part = ensemble.shape[1]
    members = ensemble.shape[2]
    chosen = jnp.take(ensemble, column_pick[0].reshape(-1), axis=0).reshape(
        window, capacity, level_part, members
    )
    blocks = []
    for slot_index in range(window):
        shift_by = slot_index - reach_tiles
        if shift_by == 0:
            blocks.append(chosen[slot_index])
        else:
            blocks.append(from_behind(chosen[slot_index], "tile", shift_by))
    arrived = jnp.stack(blocks, 0)
    slot_rows = arrived.reshape(window * capacity, level_part, members)
    columns = jnp.take(slot_rows, footprint_slot, axis=0)
    foot_rows = columns.shape[0]
    live_rows = (jnp.arange(foot_rows, dtype=jnp.int32) < footprint_count[0]).astype(jnp.float32)
    share_rows = foot_rows // lax.axis_size("chan")
    columns, sensitivity, misfit_rows = (
        lax.all_to_all(columns, "chan", split_axis=0, concat_axis=1, tiled=True),
        lax.all_to_all(jacobian, "chan", split_axis=0, concat_axis=1, tiled=True),
        lax.all_to_all(
            innovation.astype(jnp.bfloat16), "chan", split_axis=0, concat_axis=1, tiled=True
        ).astype(innovation.dtype),
    )
    response = jnp.einsum("fcl,flk->fck", sensitivity, columns, preferred_element_type=jnp.float32)
    row_weights = lax.dynamic_slice_in_dim(
        live_rows, lax.axis_index("chan") * share_rows, share_rows, 0
    )
    scales = 1.0 / jnp.sqrt(error_values)
    whitened = (
        turn_blocks(response, error_vectors) * scales[None, :, None] * row_weights[:, None, None]
    )
    misfit = turn_rows(misfit_rows, error_vectors) * scales[None, :]
    pull_sum = jnp.einsum("fck,fc->k", whitened, misfit, precision=lax.Precision.HIGHEST)
    rounded = whitened.astype(jnp.bfloat16).reshape(-1, members)
    gram_sum = lax.dot_general(
        rounded, rounded, (((0,), (0,)), ((), ())), preferred_element_type=jnp.float32
    )
    gram_sum, pull_sum = lax.psum((gram_sum, pull_sum), ("tile", "chan"))
    system = gram_sum + (members - 1) * jnp.eye(members, dtype=jnp.float32)
    factor = jnp.linalg.cholesky(system)
    halfway = lax.linalg.triangular_solve(factor, pull_sum[:, None], left_side=True, lower=True)
    mean_weights = lax.linalg.triangular_solve(
        factor, halfway, left_side=True, lower=True, transpose_a=True
    )[:, 0]
    spread = jnp.sqrt(members - 1.0) * lax.linalg.triangular_solve(
        factor, ensemble_vectors, left_side=True, lower=True, transpose_a=True
    )
    transform = (spread + mean_weights[:, None]).astype(jnp.bfloat16)
    flat_rows = ensemble.reshape(-1, members)
    updated = jnp.dot(flat_rows, transform, preferred_element_type=jnp.float32).astype(jnp.bfloat16)
    return updated.reshape(ensemble.shape)


def solution(mesh):
    return jax.shard_map(
        local,
        mesh=mesh,
        in_specs=(
            P("tile", "chan", None),
            P("tile", "chan", None),
            P("tile", "chan"),
            P(),
            P(),
            P(),
            P("tile", None, None),
            P("tile"),
            P("tile"),
        ),
        out_specs=P("tile", "chan", None),
        check_vma=False,
    )
```

profile of v0, /device:TPU:0, one launch (start us, length us, event | category | flops | bytes accessed | tf_op | source)
XLA Modules:
  0.0 357.7 jit_solution(7432755867193582582)
XLA Ops:
  7.4 5.5 %gather_fusion = bf16[200,32,256]{2,1,0:T(8,128)(2,1)} fusion(bf16[384,32,256]{2,1,0:T(8,128)(2,1)} %param.9, s32[1024]{0:T(1024)S(1)} %pad_clamp_fusion.1), kind=kCustom, calls=%fused_computation | custom fusion | bytes 6554400 | tf_op jit(solution)/shard_map/jit(_take)/gather | solution.py:47
  12.9 2.3 broadcast_select_fusion
  16.8 3.9 %collective-permute-start = (bf16[40,32,256]{2,1,0:T(8,128)(2,1)}, bf16[40,32,256]{2,1,0:T(8,128)(2,1)}, u32[]{:S(2)}, u32[]{:S(2)}) collective-permute-start(bf16[40,32,256]{2,1,0:T(8,128)(2,1)} %get-tuple-element.34), channel_id=1, source_target_pairs={{0,24},{4,28},{8,0},{12,4},{16,8},{20,12},{24,16},{28,20},{1,25},{... | collective-permute-start | bytes 1966088 | tf_op jit(solution)/shard_map/ppermute | solution.py:10
  22.7 4.9 %all-to-all-start.2 = ((bf16[4,2,640]{2,1,0:T(2,128)(2,1)}), bf16[4,2,640]{2,1,0:T(2,128)(2,1)S(1)}, u32[]{:S(2)}, u32[]{:S(2)}) async-start(bf16[4,2,640]{2,1,0:T(2,128)(2,1)} %reshape.193), calls=%async_computation.2 | async-start | bytes 20480 | tf_op jit(solution)/shard_map/all_to_all | solution.py:66
  27.6 5.6 %all-to-all-done.2 = bf16[4,2,640]{2,1,0:T(2,128)(2,1)S(1)} async-done(((bf16[4,2,640]{2,1,0:T(2,128)(2,1)}), bf16[4,2,640]{2,1,0:T(2,128)(2,1)S(1)}, u32[]{:S(2)}, u32[]{:S(2)}) %all-to-all-start.2) | async-done | bytes 10272 | tf_op jit(solution)/shard_map/all_to_all | solution.py:66
  33.2 4.3 %all-to-all-start.1 = ((bf16[160,32,128]{2,1,0:T(8,128)(2,1)}), bf16[160,32,128]{2,1,0:T(8,128)(2,1)}, u32[]{:S(2)}, u32[]{:S(2)}) async-start(bf16[160,32,128]{2,1,0:T(8,128)(2,1)} %param.10), calls=%async_computation.1 | async-start | bytes 2621440 | tf_op jit(solution)/shard_map/all_to_all | solution.py:65
  38.7 11.5 %collective-permute-done.1 = bf16[40,32,256]{2,1,0:T(8,128)(2,1)} collective-permute-done((bf16[40,32,256]{2,1,0:T(8,128)(2,1)}, bf16[40,32,256]{2,1,0:T(8,128)(2,1)}, u32[]{:S(2)}, u32[]{:S(2)}) %collective-permute-start.1) | collective-permute-done | bytes 655392 | tf_op jit(solution)/shard_map/ppermute | solution.py:10
  52.5 11.6 %collective-permute-done.3 = bf16[40,32,256]{2,1,0:T(8,128)(2,1)} collective-permute-done((bf16[40,32,256]{2,1,0:T(8,128)(2,1)}, bf16[40,32,256]{2,1,0:T(8,128)(2,1)}, u32[]{:S(2)}, u32[]{:S(2)}) %collective-permute-start.3) | collective-permute-done | bytes 655392 | tf_op jit(solution)/shard_map/ppermute | solution.py:10
  67.0 2.7 gather_fusion.1
  71.5 5.0 %all-to-all-start = ((bf16[160,32,256]{2,1,0:T(8,128)(2,1)}), bf16[160,32,256]{2,1,0:T(8,128)(2,1)S(1)}, u32[]{:S(2)}, u32[]{:S(2)}) async-start(bf16[160,32,256]{2,1,0:T(8,128)(2,1)} %broadcast_select_fusion.1), calls=%async_computation | async-start | bytes 5242880 | tf_op jit(solution)/shard_map/all_to_all | solution.py:64
  77.9 2.8 copy.24
  80.7 54.4 %all-to-all-done = bf16[160,32,256]{2,1,0:T(8,128)(2,1)S(1)} async-done(((bf16[160,32,256]{2,1,0:T(8,128)(2,1)}), bf16[160,32,256]{2,1,0:T(8,128)(2,1)S(1)}, u32[]{:S(2)}, u32[]{:S(2)}) %all-to-all-start) | async-done | bytes 2621472 | tf_op jit(solution)/shard_map/all_to_all | solution.py:64
  137.3 6.6 %multiply_convert_fusion = (bf16[40,4,32,256]{3,2,0,1:T(8,128)(2,1)S(1)}, f32[40,4,32,256]{3,2,0,1:T(8,128)}) fusion(f32[40]{0:T(128)S(1)} %dynamic_slice.3, f32[4,32]{1,0:T(4,128)S(1)} %mul.53, f32[4,32,32,1]{1,0,2,3:T(4,128)S(1)} %bitcast.144, f32[40,4,32,256]{3,2,1,0:T(8,128)S(1)} %bitcast.138), kind=kOutput, calls=%fused_computation.10 | convolution fusion | flops 507248640 | bytes 13124256 | tf_op jit(solution)/shard_map/gce,fgck->fgek/dot_general | solution.py:18
  145.8 2.9 copy.35
  149.8 2.7 fusion.45
  152.5 37.0 %psum.15 = f32[256]{0:T(256)S(1)} all-reduce(f32[256]{0:T(256)S(1)} %bitcast.148), channel_id=1, replica_groups=mesh['tile'=8,'chan'=4] {'tile','chan'}, use_global_device_ids=true, to_apply=%region_5.6 | all-reduce | flops 256 | bytes 2048 | tf_op jit(solution)/shard_map/psum | solution.py:84
  189.5 81.2 %all-reduce.3.cloned.1.call-done = f32[256,256]{0,1:T(8,128)} async-done(((f32[256,256]{0,1:T(8,128)}), f32[256,256]{0,1:T(8,128)}) %all-reduce.3.cloned.1.call-update) | async-done | bytes 262160 | tf_op jit(solution)/shard_map/psum | solution.py:84
  272.8 11.7 %cholesky.49 = f32[128,128]{1,0:T(8,128)S(1)} custom-call(f32[128,128]{1,0:T(8,128)S(1)} %cholesky.115), custom_call_target="Cholesky" | custom-call | tf_op jit(solution)/shard_map/jit(cholesky)/cholesky | solution.py:86
  284.5 9.8 %custom-call.18 = f32[1,128,128]{1,2,0:T(8,128)S(1)} custom-call(f32[1,128,128]{2,1,0:T(8,128)S(1)} %get-tuple-element.36), custom_call_target="InvertDiagBlocksLowerTriangular" | custom-call | tf_op jit(solution)/shard_map/jit(cholesky)/cholesky | solution.py:86
  294.8 11.7 %cholesky.103 = f32[128,128]{1,0:T(8,128)S(1)} custom-call(f32[128,128]{1,0:T(8,128)S(1)} %convolution_subtract_fusion.1), custom_call_target="Cholesky" | custom-call | tf_op jit(solution)/shard_map/jit(cholesky)/cholesky | solution.py:86
  308.9 4.0 %while.1 = (s32[]{:T(128)}, f32[256,256]{0,1:T(8,128)S(1)}, s32[2,2]{1,0:T(2,128)S(1)}, f32[2,128,128]{2,1,0:T(8,128)S(1)}, s32[]{:T(128)}) while((s32[]{:T(128)}, f32[256,256]{0,1:T(8,128)S(1)}, s32[2,2]{1,0:T(2,128)S(1)}, f32[2,128,128]{2,1,0:T(8,128)S(1)}, s32[]{:T(128)}) %tuple.27), condition=%wide.while_cond, body=%wide.while_body.sunk | while | flops 2 | bytes 393321 | solution.py:91
  312.9 19.9 %custom-call.19 = f32[2,128,128]{1,2,0:T(8,128)S(1)} custom-call(f32[2,128,128]{2,1,0:T(8,128)S(1)} %get-tuple-element.12), custom_call_target="InvertDiagBlocksLowerTriangular" | custom-call | tf_op jit(solution)/shard_map/triangular_solve | solution.py:91
  334.9 7.4 %fusion = bf16[12288,256]{0,1:T(8,128)(2,1)} fusion(bf16[12288,256]{1,0:T(8,128)(2,1)} %bitcast.139, f32[128,256]{1,0:T(8,128)S(1)} %fusion.23, f32[128,256]{1,0:T(8,128)S(1)} %fusion.32, f32[256]{0:T(256)S(1)} %bitcast.147), kind=kOutput, calls=%fused_computation.5 | convolution fusion | flops 1614020608 | bytes 12846080 | tf_op jit(solution)/shard_map/dot_general | solution.py:96
  342.3 8.6 %copy.38 = bf16[12288,256]{1,0:T(8,128)(2,1)} copy(bf16[12288,256]{0,1:T(8,128)(2,1)} %fusion) | data formatting | bytes 12582912 | tf_op jit(solution)/shard_map/convert_element_type | solution.py:96
  (94 shorter events, 27.9 us)
Async XLA Ops:
  15.2 6.7 %copy-start.3 = (f32[160,32]{0,1:T(8,128)S(1)}, f32[160,32]{0,1:T(8,128)}, u32[]{:S(2)}) copy-start(f32[160,32]{0,1:T(8,128)} %param.11) | copy-start | bytes 61444
  15.3 12.4 %copy-start.5 = (s32[160]{0:T(256)S(1)}, s32[160]{0:T(256)}, u32[]{:S(2)}) copy-start(s32[160]{0:T(256)} %param.16) | copy-start | bytes 1924
  16.8 20.7 %collective-permute-start = (bf16[40,32,256]{2,1,0:T(8,128)(2,1)}, bf16[40,32,256]{2,1,0:T(8,128)(2,1)}, u32[]{:S(2)}, u32[]{:S(2)}) collective-permute-start(bf16[40,32,256]{2,1,0:T(8,128)(2,1)} %get-tuple-element.34), channel_id=1, source_target_pairs={{0,24},{4,28},{8,0},{12,4},{16,8},{20,12},{24,16},{28,20},{1,25},{... | collective-permute-start | bytes 1966088 | tf_op jit(solution)/shard_map/ppermute | solution.py:10
  20.7 29.5 %collective-permute-start.1 = (bf16[40,32,256]{2,1,0:T(8,128)(2,1)}, bf16[40,32,256]{2,1,0:T(8,128)(2,1)}, u32[]{:S(2)}, u32[]{:S(2)}) collective-permute-start(bf16[40,32,256]{2,1,0:T(8,128)(2,1)} %get-tuple-element.33), channel_id=1, source_target_pairs={{0,28},{4,0},{8,4},{12,8},{16,12},{20,16},{24,20},{28,24},{1,29},{... | collective-permute-start | bytes 1966088 | tf_op jit(solution)/shard_map/ppermute | solution.py:10
  20.7 30.7 %collective-permute-start.2 = (bf16[40,32,256]{2,1,0:T(8,128)(2,1)}, bf16[40,32,256]{2,1,0:T(8,128)(2,1)}, u32[]{:S(2)}, u32[]{:S(2)}) collective-permute-start(bf16[40,32,256]{2,1,0:T(8,128)(2,1)} %get-tuple-element.32), channel_id=1, source_target_pairs={{0,4},{4,8},{8,12},{12,16},{16,20},{20,24},{24,28},{28,0},{1,5},{5... | collective-permute-start | bytes 1966088 | tf_op jit(solution)/shard_map/ppermute | solution.py:10
  21.2 42.9 %collective-permute-start.3 = (bf16[40,32,256]{2,1,0:T(8,128)(2,1)}, bf16[40,32,256]{2,1,0:T(8,128)(2,1)}, u32[]{:S(2)}, u32[]{:S(2)}) collective-permute-start(bf16[40,32,256]{2,1,0:T(8,128)(2,1)} %get-tuple-element.31), channel_id=1, source_target_pairs={{0,8},{4,12},{8,16},{12,20},{16,24},{20,28},{24,0},{28,4},{1,9},{5... | collective-permute-start | bytes 1966088 | tf_op jit(solution)/shard_map/ppermute | solution.py:10
  22.7 10.5 %all-to-all-start.2 = ((bf16[4,2,640]{2,1,0:T(2,128)(2,1)}), bf16[4,2,640]{2,1,0:T(2,128)(2,1)S(1)}, u32[]{:S(2)}, u32[]{:S(2)}) async-start(bf16[4,2,640]{2,1,0:T(2,128)(2,1)} %reshape.193), calls=%async_computation.2 | async-start | bytes 20480 | tf_op jit(solution)/shard_map/all_to_all | solution.py:66
  33.2 38.3 %all-to-all-start.1 = ((bf16[160,32,128]{2,1,0:T(8,128)(2,1)}), bf16[160,32,128]{2,1,0:T(8,128)(2,1)}, u32[]{:S(2)}, u32[]{:S(2)}) async-start(bf16[160,32,128]{2,1,0:T(8,128)(2,1)} %param.10), calls=%async_computation.1 | async-start | bytes 2621440 | tf_op jit(solution)/shard_map/all_to_all | solution.py:65
  65.2 1.7 copy-start.1
  71.5 5.7 %copy-start.6 = (f32[128]{0:T(128)S(1)}, f32[128]{0:T(128)}, u32[]{:S(2)}) copy-start(f32[128]{0:T(128)} %param.13) | copy-start | bytes 1540
  71.5 5.8 %copy-start.4 = (f32[128,32]{0,1:T(8,128)S(1)}, f32[128,32]{0,1:T(8,128)}, u32[]{:S(2)}) copy-start(f32[128,32]{0,1:T(8,128)} %param.12) | copy-start | bytes 49156
  71.5 63.6 %all-to-all-start = ((bf16[160,32,256]{2,1,0:T(8,128)(2,1)}), bf16[160,32,256]{2,1,0:T(8,128)(2,1)S(1)}, u32[]{:S(2)}, u32[]{:S(2)}) async-start(bf16[160,32,256]{2,1,0:T(8,128)(2,1)} %broadcast_select_fusion.1), calls=%async_computation | async-start | bytes 5242880 | tf_op jit(solution)/shard_map/all_to_all | solution.py:64
  76.5 194.1 %all-reduce.3.cloned.1.call-start = ((), (), s32[]{:S(2)}) async-start(), calls=%async_computation.3 | async-start | bytes 524288 | tf_op jit(solution)/shard_map/psum | solution.py:84
  135.1 1.3 copy-start
  189.5 144.6 %copy-start.2 = (f32[256,256]{1,0:T(8,128)S(1)}, f32[256,256]{1,0:T(8,128)}, u32[]{:S(2)}) copy-start(f32[256,256]{1,0:T(8,128)} %param.14) | copy-start | bytes 786436
Sparse Core Ops, SparseCore 0:
  145.9 124.6 all-reduce.2
where the time goes:
time: 359 us; the launch traced here: 358 us
  waiting for transfers between devices  164 us (46%)
  other arithmetic  61.9 us (17%)
  local copies, waits for them, and re-layouts  37.6 us (10%)
  blocking collectives  37 us (10%)
  matrix products  21.9 us (6%)
  starting transfers between devices  19.3 us (5%)
  between operations  15.6 us (4%)
    psum x1, waiting for transfers between devices, local(): gram_sum, pull_sum = lax.psum((gram_sum, pull_sum), ('tile', 'chan'))  81.2 us
    all_to_all x1, waiting for transfers between devices, local(): lax.all_to_all(columns, 'chan', split_axis=0, concat_axis=1, tiled=True)  54.4 us
    psum x1, blocking collectives, local(): gram_sum, pull_sum = lax.psum((gram_sum, pull_sum), ('tile', 'chan'))  37 us
    another operation x6, other arithmetic, local(): factor = jnp.linalg.cholesky(system)  33.9 us
    ppermute x4, waiting for transfers between devices, from_behind(): return lax.ppermute(value, axis, pairs)  23.1 us
    another operation x3, other arithmetic, local(): lax.linalg.triangular_solve(factor, ensemble_vectors, left_side=True, low...  20 us
    convert_element_type x1, local copies, waits for them, and re-layouts, local(): jnp.dot(flat_rows, transform, preferred_element_type=jnp.float32)  8.6 us
    dot_general x1, matrix products, local(): jnp.dot(flat_rows, transform, preferred_element_type=jnp.float32)  7.38 us
  transfers between devices with their start and end apart: 8, of which 5 were waited for; matrix products, arithmetic and copies ran while one was open for 6% of the time, Pallas kernels for 0%

commit v1 on v0

--- a/solution.py
+++ b/solution.py
@@ -81,7 +81,7 @@
     gram_sum = lax.dot_general(
         rounded, rounded, (((0,), (0,)), ((), ())), preferred_element_type=jnp.float32
     )
-    gram_sum, pull_sum = lax.psum((gram_sum, pull_sum), ("tile", "chan"))
+    gram_sum, pull_sum = lax.psum(lax.psum((gram_sum, pull_sum), "tile"), "chan")
     system = gram_sum + (members - 1) * jnp.eye(members, dtype=jnp.float32)
     factor = jnp.linalg.cholesky(system)
     halfway = lax.linalg.triangular_solve(factor, pull_sum[:, None], left_side=True, lower=True)

time: 359 us -> 324 us (0.903)
  waiting for transfers between devices: 164 us -> 137 us
  blocking collectives: 37 us -> 24 us
    psum x1 -> x2, waiting for transfers between devices: 81.2 us -> 54.2 us  [the longest x1 45.5 us: local(): lax.psum((gram_sum, pull_sum), 'tile')]
    psum x1 -> x2, blocking collectives: 37 us -> 24 us  [the longest x1 12.2 us: local(): lax.psum(lax.psum((gram_sum, pull_sum), 'tile'), 'chan')]
  transfers between devices with their start and end apart: 8 -> 9, of which waited for: 5 -> 6; matrix products, arithmetic and copies ran while one was open for 6% -> 8% of each run, Pallas kernels for 0% -> 0%
where the time goes in v1:
time: 324 us; the launch traced here: 323 us
  waiting for transfers between devices  137 us (42%)
  other arithmetic  64.6 us (20%)
  local copies, waits for them, and re-layouts  37.8 us (12%)
  blocking collectives  24 us (7%)
  matrix products  23.7 us (7%)
  starting transfers between devices  19.3 us (6%)
  between operations  15.7 us (5%)
    all_to_all x1, waiting for transfers between devices, local(): lax.all_to_all(columns, 'chan', split_axis=0, concat_axis=1, tiled=True)  54.4 us
    psum x1, waiting for transfers between devices, local(): lax.psum((gram_sum, pull_sum), 'tile')  45.5 us
    another operation x6, other arithmetic, local(): factor = jnp.linalg.cholesky(system)  34 us
    ppermute x4, waiting for transfers between devices, from_behind(): return lax.ppermute(value, axis, pairs)  23.1 us
    another operation x3, other arithmetic, local(): lax.linalg.triangular_solve(factor, ensemble_vectors, left_side=True, low...  19.9 us
    psum x1, blocking collectives, local(): lax.psum(lax.psum((gram_sum, pull_sum), 'tile'), 'chan')  12.2 us
    psum x1, blocking collectives, local(): lax.psum((gram_sum, pull_sum), 'tile')  11.8 us
    psum x1, waiting for transfers between devices, local(): lax.psum(lax.psum((gram_sum, pull_sum), 'tile'), 'chan')  8.72 us
  transfers between devices with their start and end apart: 9, of which 6 were waited for; matrix products, arithmetic and copies ran while one was open for 8% of the time, Pallas kernels for 0%

profile of v1, /device:TPU:0, one launch (start us, length us, event | category | flops | bytes accessed | tf_op | source)
XLA Modules:
  0.0 322.5 jit_solution(14947929338174270441)
XLA Ops:
  7.4 5.5 %gather_fusion = bf16[200,32,256]{2,1,0:T(8,128)(2,1)} fusion(bf16[384,32,256]{2,1,0:T(8,128)(2,1)} %param.9, s32[1024]{0:T(1024)S(1)} %pad_clamp_fusion.1), kind=kCustom, calls=%fused_computation | custom fusion | bytes 6554400 | tf_op jit(solution)/shard_map/jit(_take)/gather | solution.py:47
  16.8 3.9 %collective-permute-start = (bf16[40,32,256]{2,1,0:T(8,128)(2,1)}, bf16[40,32,256]{2,1,0:T(8,128)(2,1)}, u32[]{:S(2)}, u32[]{:S(2)}) collective-permute-start(bf16[40,32,256]{2,1,0:T(8,128)(2,1)} %get-tuple-element.34), channel_id=1, source_target_pairs={{0,24},{4,28},{8,0},{12,4},{16,8},{20,12},{24,16},{28,20},{1,25},{... | collective-permute-start | bytes 1966088 | tf_op jit(solution)/shard_map/ppermute | solution.py:10
  22.7 4.9 %all-to-all-start.2 = ((bf16[4,2,640]{2,1,0:T(2,128)(2,1)}), bf16[4,2,640]{2,1,0:T(2,128)(2,1)S(1)}, u32[]{:S(2)}, u32[]{:S(2)}) async-start(bf16[4,2,640]{2,1,0:T(2,128)(2,1)} %reshape.193), calls=%async_computation.2 | async-start | bytes 20480 | tf_op jit(solution)/shard_map/all_to_all | solution.py:66
  27.6 5.6 %all-to-all-done.2 = bf16[4,2,640]{2,1,0:T(2,128)(2,1)S(1)} async-done(((bf16[4,2,640]{2,1,0:T(2,128)(2,1)}), bf16[4,2,640]{2,1,0:T(2,128)(2,1)S(1)}, u32[]{:S(2)}, u32[]{:S(2)}) %all-to-all-start.2) | async-done | bytes 10272 | tf_op jit(solution)/shard_map/all_to_all | solution.py:66
  33.2 4.3 %all-to-all-start.1 = ((bf16[160,32,128]{2,1,0:T(8,128)(2,1)}), bf16[160,32,128]{2,1,0:T(8,128)(2,1)}, u32[]{:S(2)}, u32[]{:S(2)}) async-start(bf16[160,32,128]{2,1,0:T(8,128)(2,1)} %param.10), calls=%async_computation.1 | async-start | bytes 2621440 | tf_op jit(solution)/shard_map/all_to_all | solution.py:65
  38.7 11.5 %collective-permute-done.1 = bf16[40,32,256]{2,1,0:T(8,128)(2,1)} collective-permute-done((bf16[40,32,256]{2,1,0:T(8,128)(2,1)}, bf16[40,32,256]{2,1,0:T(8,128)(2,1)}, u32[]{:S(2)}, u32[]{:S(2)}) %collective-permute-start.1) | collective-permute-done | bytes 655392 | tf_op jit(solution)/shard_map/ppermute | solution.py:10
  52.5 11.6 %collective-permute-done.3 = bf16[40,32,256]{2,1,0:T(8,128)(2,1)} collective-permute-done((bf16[40,32,256]{2,1,0:T(8,128)(2,1)}, bf16[40,32,256]{2,1,0:T(8,128)(2,1)}, u32[]{:S(2)}, u32[]{:S(2)}) %collective-permute-start.3) | collective-permute-done | bytes 655392 | tf_op jit(solution)/shard_map/ppermute | solution.py:10
  71.5 5.0 %all-to-all-start = ((bf16[160,32,256]{2,1,0:T(8,128)(2,1)}), bf16[160,32,256]{2,1,0:T(8,128)(2,1)S(1)}, u32[]{:S(2)}, u32[]{:S(2)}) async-start(bf16[160,32,256]{2,1,0:T(8,128)(2,1)} %broadcast_select_fusion.1), calls=%async_computation | async-start | bytes 5242880 | tf_op jit(solution)/shard_map/all_to_all | solution.py:64
  80.7 54.4 %all-to-all-done = bf16[160,32,256]{2,1,0:T(8,128)(2,1)S(1)} async-done(((bf16[160,32,256]{2,1,0:T(8,128)(2,1)}), bf16[160,32,256]{2,1,0:T(8,128)(2,1)S(1)}, u32[]{:S(2)}, u32[]{:S(2)}) %all-to-all-start) | async-done | bytes 2621472 | tf_op jit(solution)/shard_map/all_to_all | solution.py:64
  137.3 6.6 %multiply_convert_fusion = (bf16[40,4,32,256]{3,2,0,1:T(8,128)(2,1)S(1)}, f32[40,4,32,256]{3,2,0,1:T(8,128)}) fusion(f32[40]{0:T(128)S(1)} %dynamic_slice.3, f32[4,32]{1,0:T(4,128)S(1)} %mul.53, f32[4,32,32,1]{1,0,2,3:T(4,128)S(1)} %bitcast.144, f32[40,4,32,256]{3,2,1,0:T(8,128)S(1)} %bitcast.138), kind=kOutput, calls=%fused_computation.10 | convolution fusion | flops 507248640 | bytes 13124256 | tf_op jit(solution)/shard_map/gce,fgck->fgek/dot_general | solution.py:18
  145.9 2.9 copy.35
  148.8 3.7 %fusion.1 = f32[40,128,256]{2,1,0:T(8,128)} fusion(f32[40,4,32,256]{3,2,1,0:T(8,128)S(1)} %copy.35, f32[40]{0:T(128)S(1)} %dynamic_slice.3, f32[128]{0:T(128)S(1)} %sqrt.3), kind=kLoop, calls=%fused_computation.7 | loop fusion | flops 2621440 | bytes 10486432 | tf_op jit(solution)/shard_map/mul | solution.py:76
  152.5 45.5 %all-reduce.4.cloned.1.call-done = f32[256,256]{0,1:T(8,128)} async-done(((f32[256,256]{0,1:T(8,128)}), f32[256,256]{0,1:T(8,128)}) %all-reduce.4.cloned.1.call-update) | async-done | bytes 262160 | tf_op jit(solution)/shard_map/psum | solution.py:84
  198.1 4.4 %fusion.45 = f32[1,256,1]{1,0,2:T(1,128)S(1)} fusion(f32[40,128,256]{2,1,0:T(8,128)} %fusion.1, f32[40,128,1]{1,2,0:T(1,128)S(1)} %copy.43), kind=kOutput, calls=%fused_computation.90 | convolution fusion | flops 15728640 | bytes 5264384 | tf_op jit(solution)/shard_map/fck,fc->k/dot_general | solution.py:79
  202.5 11.8 %psum.30 = f32[256]{0:T(256)S(1)} all-reduce(f32[256]{0:T(256)S(1)} %bitcast.148), channel_id=1, replica_groups=mesh['tile'=8,'chan'=4] {'tile'}, use_global_device_ids=true, to_apply=%region_6.7 | all-reduce | flops 256 | bytes 2048 | tf_op jit(solution)/shard_map/psum | solution.py:84
  214.2 12.2 %psum.31 = f32[256]{0:T(256)S(1)} all-reduce(f32[256]{0:T(256)S(1)} %psum.30), channel_id=1, replica_groups=mesh['tile'=8,'chan'=4] {'chan'}, use_global_device_ids=true, to_apply=%region_7.8 | all-reduce | flops 256 | bytes 2048 | tf_op jit(solution)/shard_map/psum | solution.py:84
  226.5 8.7 %all-reduce.6.cloned.1.call-done = f32[256,256]{0,1:T(8,128)} async-done(((f32[256,256]{0,1:T(8,128)}), f32[256,256]{0,1:T(8,128)}) %all-reduce.6.cloned.1.call-update) | async-done | bytes 262160 | tf_op jit(solution)/shard_map/psum | solution.py:84
  237.3 11.7 %cholesky.49 = f32[128,128]{1,0:T(8,128)S(1)} custom-call(f32[128,128]{1,0:T(8,128)S(1)} %cholesky.115), custom_call_target="Cholesky" | custom-call | tf_op jit(solution)/shard_map/jit(cholesky)/cholesky | solution.py:86
  249.1 9.8 %custom-call.18 = f32[1,128,128]{1,2,0:T(8,128)S(1)} custom-call(f32[1,128,128]{2,1,0:T(8,128)S(1)} %get-tuple-element.36), custom_call_target="InvertDiagBlocksLowerTriangular" | custom-call | tf_op jit(solution)/shard_map/jit(cholesky)/cholesky | solution.py:86
  259.4 11.7 %cholesky.103 = f32[128,128]{1,0:T(8,128)S(1)} custom-call(f32[128,128]{1,0:T(8,128)S(1)} %convolution_subtract_fusion.1), custom_call_target="Cholesky" | custom-call | tf_op jit(solution)/shard_map/jit(cholesky)/cholesky | solution.py:86
  273.6 4.2 %while.1 = (s32[]{:T(128)}, f32[256,256]{0,1:T(8,128)S(1)}, s32[2,2]{1,0:T(2,128)S(1)}, f32[2,128,128]{2,1,0:T(8,128)S(1)}, s32[]{:T(128)}) while((s32[]{:T(128)}, f32[256,256]{0,1:T(8,128)S(1)}, s32[2,2]{1,0:T(2,128)S(1)}, f32[2,128,128]{2,1,0:T(8,128)S(1)}, s32[]{:T(128)}) %tuple.27), condition=%wide.while_cond, body=%wide.while_body.sunk | while | flops 2 | bytes 393321 | solution.py:91
  277.8 19.9 %custom-call.19 = f32[2,128,128]{1,2,0:T(8,128)S(1)} custom-call(f32[2,128,128]{2,1,0:T(8,128)S(1)} %get-tuple-element.12), custom_call_target="InvertDiagBlocksLowerTriangular" | custom-call | tf_op jit(solution)/shard_map/triangular_solve | solution.py:91
  299.7 7.4 %fusion = bf16[12288,256]{0,1:T(8,128)(2,1)} fusion(bf16[12288,256]{1,0:T(8,128)(2,1)} %bitcast.139, f32[128,256]{1,0:T(8,128)S(1)} %fusion.23, f32[128,256]{1,0:T(8,128)S(1)} %fusion.32, f32[256]{0:T(256)S(1)} %bitcast.147), kind=kOutput, calls=%fused_computation.5 | convolution fusion | flops 1614020608 | bytes 12846080 | tf_op jit(solution)/shard_map/dot_general | solution.py:96
  307.1 8.6 %copy.38 = bf16[12288,256]{1,0:T(8,128)(2,1)} copy(bf16[12288,256]{0,1:T(8,128)(2,1)} %fusion) | data formatting | bytes 12582912 | tf_op jit(solution)/shard_map/convert_element_type | solution.py:96
  (98 shorter events, 35.1 us)
Async XLA Ops:
  15.2 6.7 %copy-start.3 = (f32[160,32]{0,1:T(8,128)S(1)}, f32[160,32]{0,1:T(8,128)}, u32[]{:S(2)}) copy-start(f32[160,32]{0,1:T(8,128)} %param.11) | copy-start | bytes 61444
  15.3 12.4 %copy-start.5 = (s32[160]{0:T(256)S(1)}, s32[160]{0:T(256)}, u32[]{:S(2)}) copy-start(s32[160]{0:T(256)} %param.16) | copy-start | bytes 1924
  16.8 20.7 %collective-permute-start = (bf16[40,32,256]{2,1,0:T(8,128)(2,1)}, bf16[40,32,256]{2,1,0:T(8,128)(2,1)}, u32[]{:S(2)}, u32[]{:S(2)}) collective-permute-start(bf16[40,32,256]{2,1,0:T(8,128)(2,1)} %get-tuple-element.34), channel_id=1, source_target_pairs={{0,24},{4,28},{8,0},{12,4},{16,8},{20,12},{24,16},{28,20},{1,25},{... | collective-permute-start | bytes 1966088 | tf_op jit(solution)/shard_map/ppermute | solution.py:10
  20.7 29.5 %collective-permute-start.1 = (bf16[40,32,256]{2,1,0:T(8,128)(2,1)}, bf16[40,32,256]{2,1,0:T(8,128)(2,1)}, u32[]{:S(2)}, u32[]{:S(2)}) collective-permute-start(bf16[40,32,256]{2,1,0:T(8,128)(2,1)} %get-tuple-element.33), channel_id=1, source_target_pairs={{0,28},{4,0},{8,4},{12,8},{16,12},{20,16},{24,20},{28,24},{1,29},{... | collective-permute-start | bytes 1966088 | tf_op jit(solution)/shard_map/ppermute | solution.py:10
  20.7 30.7 %collective-permute-start.2 = (bf16[40,32,256]{2,1,0:T(8,128)(2,1)}, bf16[40,32,256]{2,1,0:T(8,128)(2,1)}, u32[]{:S(2)}, u32[]{:S(2)}) collective-permute-start(bf16[40,32,256]{2,1,0:T(8,128)(2,1)} %get-tuple-element.32), channel_id=1, source_target_pairs={{0,4},{4,8},{8,12},{12,16},{16,20},{20,24},{24,28},{28,0},{1,5},{5... | collective-permute-start | bytes 1966088 | tf_op jit(solution)/shard_map/ppermute | solution.py:10
  21.2 42.9 %collective-permute-start.3 = (bf16[40,32,256]{2,1,0:T(8,128)(2,1)}, bf16[40,32,256]{2,1,0:T(8,128)(2,1)}, u32[]{:S(2)}, u32[]{:S(2)}) collective-permute-start(bf16[40,32,256]{2,1,0:T(8,128)(2,1)} %get-tuple-element.31), channel_id=1, source_target_pairs={{0,8},{4,12},{8,16},{12,20},{16,24},{20,28},{24,0},{28,4},{1,9},{5... | collective-permute-start | bytes 1966088 | tf_op jit(solution)/shard_map/ppermute | solution.py:10
  22.7 10.5 %all-to-all-start.2 = ((bf16[4,2,640]{2,1,0:T(2,128)(2,1)}), bf16[4,2,640]{2,1,0:T(2,128)(2,1)S(1)}, u32[]{:S(2)}, u32[]{:S(2)}) async-start(bf16[4,2,640]{2,1,0:T(2,128)(2,1)} %reshape.193), calls=%async_computation.2 | async-start | bytes 20480 | tf_op jit(solution)/shard_map/all_to_all | solution.py:66
  33.2 38.3 %all-to-all-start.1 = ((bf16[160,32,128]{2,1,0:T(8,128)(2,1)}), bf16[160,32,128]{2,1,0:T(8,128)(2,1)}, u32[]{:S(2)}, u32[]{:S(2)}) async-start(bf16[160,32,128]{2,1,0:T(8,128)(2,1)} %param.10), calls=%async_computation.1 | async-start | bytes 2621440 | tf_op jit(solution)/shard_map/all_to_all | solution.py:65
  65.3 1.7 copy-start.1
  71.5 5.7 %copy-start.6 = (f32[128]{0:T(128)S(1)}, f32[128]{0:T(128)}, u32[]{:S(2)}) copy-start(f32[128]{0:T(128)} %param.13) | copy-start | bytes 1540
  71.5 5.8 %copy-start.4 = (f32[128,32]{0,1:T(8,128)S(1)}, f32[128,32]{0,1:T(8,128)}, u32[]{:S(2)}) copy-start(f32[128,32]{0,1:T(8,128)} %param.12) | copy-start | bytes 49156
  71.5 63.6 %all-to-all-start = ((bf16[160,32,256]{2,1,0:T(8,128)(2,1)}), bf16[160,32,256]{2,1,0:T(8,128)(2,1)S(1)}, u32[]{:S(2)}, u32[]{:S(2)}) async-start(bf16[160,32,256]{2,1,0:T(8,128)(2,1)} %broadcast_select_fusion.1), calls=%async_computation | async-start | bytes 5242880 | tf_op jit(solution)/shard_map/all_to_all | solution.py:64
  76.5 121.5 %all-reduce.4.cloned.1.call-start = ((), (), s32[]{:S(2)}) async-start(), calls=%async_computation.3 | async-start | bytes 524288 | tf_op jit(solution)/shard_map/psum | solution.py:84
  135.1 1.3 copy-start
  145.8 89.4 %all-reduce.6.cloned.1.call-start = ((), (), s32[]{:S(2)}) async-start(), calls=%async_computation.4 | async-start | bytes 524288 | tf_op jit(solution)/shard_map/psum | solution.py:84
  226.5 72.4 %copy-start.2 = (f32[256,256]{1,0:T(8,128)S(1)}, f32[256,256]{1,0:T(8,128)}, u32[]{:S(2)}) copy-start(f32[256,256]{1,0:T(8,128)} %param.14) | copy-start | bytes 786436
Sparse Core Ops, SparseCore 0:
  145.9 52.0 all-reduce.3
  200.4 34.7 all-reduce.5
